TPU v7x, 32 devices: a whole 2x2x4 slice. The times are simulated.
32 devices in a mesh: leaf: 8 (over z, x), vec: 4 (over y, core).
Axes of the slice: x: 2, y: 2, z: 4, core: 2. Of those that a mesh axis runs over, the one named last changes fastest.
Arguments:
- vectors: float32 [32, 65536], P('vec', 'leaf'), may hold values from -15 to 15
- coords: float32 [3, 65536], P(None, 'leaf'), may hold values from 0 to 64, as said below
- leaf_basis: float32 [32, 65536], P(None, 'leaf'), may hold values from -0.375 to 0.375
- node_ops: float32 [496, 32, 128], P('leaf'), may hold values from -0.75 to 0.75
- top_ops: float32 [2, 32, 192], replicated, may hold values from -0.75 to 0.75
- near_target: int32 [1280], P('leaf'), may hold values from 0 to 255, as said below
- near_source: int32 [1280], P('leaf'), may hold values from 0 to 255, as said below
- near_count: int32 [8], P('leaf'), may hold values from 64 to 160, as said below
Outputs:
- product: float32 [32, 65536], P('vec', 'leaf')
- gram_matrix: float32 [32, 32], P(None, 'vec')
Inputs may be any that keep to these rules, and one draw needn't show every extreme that they name: `near_target`: slots of one index of leaf name target leaves of that index only; each aligned block of 32 slots of an index names each of its leaves once; in the first run every leaf is paired with itself, and in the second run the first leaf of each index is paired with the leaf just below it and the last leaf with the leaf just above it, where those exist. `near_source`: A source leaf lies within 4 leaves of its target leaf; no pair repeats within one index of leaf. The first near_count[d] slots of index d are live, the rest are padding; some index fills all 160 slots. `coords`: point k lies in the box of its leaf l = k // 256: first coordinate from 0.25 l to 0.25 (l + 1), the other two from 0 to 1.
All inputs are finite; a program needn't handle non-finite values.
Results may differ from a plain program's by a relative error of at most 0.0003.
Values sent between devices are 32-bit elements; how exact they have to be, the bound alone decides.
A program may use at most 64 MiB of HBM per device.

v0:
```python
import jax
import jax.numpy as jnp
import numpy as np
from jax import lax
from jax.sharding import PartitionSpec as P

PTS = 256
NEAR_REACH = 4
EXACT_ARITHMETIC = lax.Precision.HIGHEST
SIGNAL = 0.1
NUGGET = 0.5
LENGTH = 0.35
EVEN_OFFSETS = (-2, 2, 3)
ODD_OFFSETS = (-3, -2, 2)


def padded_2(block, sides, width):
    for axis, dim in sides:
        count = lax.axis_size(axis)
        forward = [(i, i + 1) for i in range(count - 1)]
        backward = [(target, source) for source, target in forward]
        low = lax.ppermute(
            lax.slice_in_dim(block, block.shape[dim] - width, None, axis=dim), axis, forward
        )
        high = lax.ppermute(lax.slice_in_dim(block, 0, width, axis=dim), axis, backward)
        block = jnp.concatenate([low, block, high], axis=dim)
    return block


def matern(target_pts, source_pts):
    pair_separation = jnp.zeros(
        (target_pts.shape[1], target_pts.shape[2], source_pts.shape[2]), jnp.float32
    )
    for axis_id in range(3):
        spacing = target_pts[axis_id][:, :, None] - source_pts[axis_id][:, None, :]
        pair_separation = pair_separation + spacing * spacing
    scaled = jnp.sqrt(3.0 * pair_separation) / LENGTH
    return SIGNAL * (1.0 + scaled) * jnp.exp(-scaled)


def take_rows(padded, count_nodes, pad_width):
    parity_ids = np.arange(count_nodes) % 2
    gathered = []
    for slot_index in range(3):
        shift_by = np.where(parity_ids == 0, EVEN_OFFSETS[slot_index], ODD_OFFSETS[slot_index])
        gathered.append(padded[np.arange(count_nodes) + shift_by + pad_width])
    return jnp.stack(gathered, axis=1)


def couple_level(padded, operators, count_nodes, pad_width, rank_size):
    sources = take_rows(padded, count_nodes, pad_width)
    blocks = operators[:, :, : 3 * rank_size].reshape(count_nodes, rank_size, 3, rank_size)
    return jnp.einsum("navr,nras->nvs", sources, blocks, precision=EXACT_ARITHMETIC)


def raise_level(incoming_coefficients, operators, rank_size):
    moved = jnp.einsum(
        "nvr,nrs->nvs",
        incoming_coefficients,
        operators[:, :, 3 * rank_size :],
        precision=EXACT_ARITHMETIC,
    )
    return moved[0::2] + moved[1::2]


def lower_level(field_in, operators, rank_size):
    spread = jnp.repeat(field_in, 2, axis=0)
    return jnp.einsum(
        "nvs,nrs->nvr", spread, operators[:, :, 3 * rank_size :], precision=EXACT_ARITHMETIC
    )


def through(incoming_coefficients, operators, position, rank_size):
    return jnp.einsum(
        "...r,rs->...s",
        incoming_coefficients,
        operators[:, position * rank_size : (position + 1) * rank_size],
        precision=EXACT_ARITHMETIC,
    )


def couple_top(partners, operators, parity, rank_size):
    far_left, near_left, near_right, far_right = partners
    outer = jnp.where(
        parity == 0,
        through(far_right, operators, 3, rank_size),
        through(far_left, operators, 0, rank_size),
    )
    return (
        through(near_left, operators, 1, rank_size)
        + through(near_right, operators, 2, rank_size)
        + outer
    )


def raise_pair(left_coef, right_coef, operators, rank_size):
    return through(left_coef, operators, 4, rank_size) + through(
        right_coef, operators, 5, rank_size
    )


def lower_top(field_in, operators, parity, rank_size):
    even_part = jnp.einsum(
        "...s,rs->...r",
        field_in,
        operators[:, 4 * rank_size : 5 * rank_size],
        precision=EXACT_ARITHMETIC,
    )
    odd_part = jnp.einsum(
        "...s,rs->...r",
        field_in,
        operators[:, 5 * rank_size : 6 * rank_size],
        precision=EXACT_ARITHMETIC,
    )
    return jnp.where(parity == 0, even_part, odd_part)


def near_field(window, local_coords, targets, sources, weights, pair_block):
    columns = window.shape[0] - 3
    leaves_dev = local_coords.shape[1]
    step_count = targets.shape[0] // pair_block

    def add_block(accumulated_sum, portion):
        target_ids, source_ids, live_mask = portion
        source_rows = jnp.take(window, source_ids, axis=1)
        target_pts = jnp.take(local_coords, target_ids, axis=1)
        kernel = matern(target_pts, source_rows[columns:])
        contribution = jnp.einsum(
            "vbs,bts->bvt", source_rows[:columns], kernel, precision=EXACT_ARITHMETIC
        )
        selection_mask = (target_ids[:, None] == jnp.arange(leaves_dev)[None, :]).astype(
            jnp.float32
        ) * live_mask[:, None]
        return (
            accumulated_sum
            + jnp.einsum("qs,qhg->hsg", selection_mask, contribution, precision=EXACT_ARITHMETIC),
            None,
        )

    initial = jnp.zeros((columns, leaves_dev, window.shape[2]), jnp.float32)
    portions = (
        targets.reshape(step_count, pair_block),
        sources.reshape(step_count, pair_block),
        weights.reshape(step_count, pair_block),
    )
    accumulated_sum, unused = lax.scan(add_block, initial, portions)
    return accumulated_sum.reshape(columns, leaves_dev * window.shape[2])


def on_device(vectors, coords, leaf_basis, node_ops, top_ops, near_target, near_source, near_count):
    rank_size = leaf_basis.shape[0]
    columns_dev = vectors.shape[0]
    points_dev = vectors.shape[1]
    leaves_dev = points_dev // PTS
    device = lax.axis_index("leaf")
    vec_index = lax.axis_index("vec")
    vec_count = lax.axis_size("vec")
    leaf_count = lax.axis_size("leaf")
    all_columns = lax.all_gather(vectors, "vec", axis=0, tiled=True)
    base_leaf = device * leaves_dev
    slot_ids = jnp.arange(near_target.shape[0], dtype=jnp.int32)
    live_all = (slot_ids < near_count[0]).astype(jnp.float32)
    target_all = near_target - base_leaf
    source_all = near_source - base_leaf + NEAR_REACH
    local_coords = coords.reshape(3, leaves_dev, PTS)
    stacked = jnp.concatenate([all_columns, coords], axis=0)
    window = padded_2(stacked, (("leaf", 1),), NEAR_REACH * PTS)
    window = window.reshape(all_columns.shape[0] + 3, leaves_dev + 2 * NEAR_REACH, PTS)
    share_count = near_target.shape[0] // vec_count
    slot_grid = slot_ids.reshape(share_count, vec_count)
    picked = lax.dynamic_slice_in_dim(slot_grid, vec_index, 1, 1)[:, 0]
    partial_sum = near_field(
        window,
        local_coords,
        target_all[picked],
        source_all[picked],
        live_all[picked],
        share_count // (leaves_dev // vec_count),
    )
    near_part = lax.psum_scatter(partial_sum, "vec", scatter_dimension=0, tiled=True)
    leaf_basis_matrix = leaf_basis.reshape(rank_size, leaves_dev, PTS)
    current = jnp.einsum(
        "vlp,rlp->lvr",
        vectors.reshape(columns_dev, leaves_dev, PTS),
        leaf_basis_matrix,
        precision=EXACT_ARITHMETIC,
    )
    level_ops = []
    level_fields = []
    offset_node = 0
    nodes_here = leaves_dev
    while nodes_here >= 2:
        ops_here = node_ops[offset_node : offset_node + nodes_here]
        rim_width = min(3, nodes_here)
        padded = padded_2(current, (("leaf", 0),), rim_width)
        level_fields.append(couple_level(padded, ops_here, nodes_here, rim_width, rank_size))
        level_ops.append(ops_here)
        current = raise_level(current, ops_here, rank_size)
        offset_node += nodes_here
        nodes_here //= 2
    top_levels = top_ops.shape[0]
    top_fields = []
    all_roots = lax.all_gather(current, "leaf", axis=0, tiled=True)
    for height in range(top_levels):
        padded_top = jnp.pad(all_roots, ((3, 3), (0, 0), (0, 0)))
        node_id = device // (1 << height)
        near_rows = lax.dynamic_slice_in_dim(padded_top, node_id, 7, 0)
        partners = (near_rows[0], near_rows[1], near_rows[5], near_rows[6])
        top_fields.append(couple_top(partners, top_ops[height], node_id % 2, rank_size))
        if height + 1 < top_levels:
            all_roots = raise_pair(all_roots[0::2], all_roots[1::2], top_ops[height], rank_size)
    downward = top_fields[top_levels - 1]
    for height in range(top_levels - 2, -1, -1):
        parity = device // (1 << height) % 2
        downward = top_fields[height] + lower_top(downward, top_ops[height], parity, rank_size)
    downward = downward[None]
    for index_level in range(len(level_fields) - 1, -1, -1):
        downward = level_fields[index_level] + lower_level(
            downward, level_ops[index_level], rank_size
        )
    far_part = jnp.einsum(
        "lvr,rlp->vlp", downward, leaf_basis_matrix, precision=EXACT_ARITHMETIC
    ).reshape(columns_dev, points_dev)
    product = near_part + far_part + NUGGET * vectors
    gram_part = jnp.einsum("ip,jp->ij", all_columns, product, precision=EXACT_ARITHMETIC)
    gram_matrix = lax.psum(gram_part, "leaf") / (leaf_count * points_dev)
    return (product, gram_matrix)


def solution(mesh):
    return jax.shard_map(
        on_device,
        mesh=mesh,
        in_specs=(
            P("vec", "leaf"),
            P(None, "leaf"),
            P(None, "leaf"),
            P("leaf", None, None),
            P(),
            P("leaf"),
            P("leaf"),
            P("leaf"),
        ),
        out_specs=(P("vec", "leaf"), P(None, "vec")),
        check_vma=False,
    )
```

profile of v0, /device:TPU:0, one launch (start us, length us, event | category | flops | bytes accessed | tf_op | source)
XLA Modules:
  0.0 216.0 jit_solution(17568019953974837203)
XLA Ops:
  7.2 2.3 %fusion.55 = f32[32,8,32]{2,1,0:T(8,128)S(1)} fusion(f32[8,32,256]{2,0,1:T(8,128)} %bitcast.178, f32[4,32,8,256]{3,2,1,0:T(8,128)} %bitcast.175), kind=kOutput, calls=%fused_computation.110 | convolution fusion | flops 25165824 | bytes 1343488 | tf_op jit(solution)/shard_map/vlp,rlp->lvr/dot_general | solution.py:182
  11.4 4.9 %collective-permute-start.10 = (f32[2,8,32]{2,1,0:T(8,128)S(1)}, f32[2,8,32]{2,1,0:T(8,128)S(1)}, u32[]{:S(2)}, u32[]{:S(2)}) collective-permute-start(f32[2,8,32]{2,1,0:T(8,128)S(1)} %slice_add_fusion.3), channel_id=1, source_target_pairs={{0,4},{4,8},{8,12},{12,16},{16,20},{20,24},{24,28},{1,5},{5,9},{9,... | collective-permute-start | bytes 6152 | tf_op jit(solution)/shard_map/ppermute | solution.py:22
  18.3 5.1 %collective-permute-start.8 = (f32[3,8,32]{2,1,0:T(8,128)}, f32[3,8,32]{2,1,0:T(8,128)}, u32[]{:S(2)}, u32[]{:S(2)}) collective-permute-start(f32[3,8,32]{2,1,0:T(8,128)} %get-tuple-element.113), channel_id=1, source_target_pairs={{0,4},{4,8},{8,12},{12,16},{16,20},{20,24},{24,28},{1,5},{5,9},{9,... | collective-permute-start | bytes 9224 | tf_op jit(solution)/shard_map/ppermute | solution.py:22
  24.0 4.4 %collective-permute-start.6 = (f32[3,8,32]{2,1,0:T(8,128)}, f32[3,8,32]{2,1,0:T(8,128)}, u32[]{:S(2)}, u32[]{:S(2)}) collective-permute-start(f32[3,8,32]{2,1,0:T(8,128)} %get-tuple-element.111), channel_id=1, source_target_pairs={{0,4},{4,8},{8,12},{12,16},{16,20},{20,24},{24,28},{1,5},{5,9},{9,... | collective-permute-start | bytes 9224 | tf_op jit(solution)/shard_map/ppermute | solution.py:22
  29.9 31.5 %all_gather.7 = f32[8,8,32]{2,1,0:T(8,128)S(1)} all-gather(f32[1,8,32]{2,1,0:T(8,128)S(1)} %slice_add_fusion.4), channel_id=1, replica_groups=mesh['leaf'=8,'vec'=4] {'leaf'}, dimensions={0}, use_global_device_ids=true | all-gather | bytes 9216 | tf_op jit(solution)/shard_map/all_gather | solution.py:203
  74.0 1.7 reshape.157
  78.4 1.6 collective-permute-start.4
  84.9 4.6 %collective-permute-start = (f32[35,1024]{1,0:T(8,128)S(1)}, f32[35,1024]{1,0:T(8,128)S(1)}, u32[]{:S(2)}, u32[]{:S(2)}) collective-permute-start(f32[35,1024]{1,0:T(8,128)S(1)} %get-tuple-element.103), channel_id=1, source_target_pairs={{0,4},{4,8},{8,12},{12,16},{16,20},{20,24},{24,28},{1,5},{5,9},{9,... | collective-permute-start | bytes 430088 | tf_op jit(solution)/shard_map/ppermute | solution.py:22
  92.9 5.2 %collective-permute-start.2 = (f32[3,8,32]{2,1,0:T(8,128)}, f32[3,8,32]{2,1,0:T(8,128)S(1)}, u32[]{:S(2)}, u32[]{:S(2)}) collective-permute-start(f32[3,8,32]{2,1,0:T(8,128)} %get-tuple-element.105), channel_id=1, source_target_pairs={{0,4},{4,8},{8,12},{12,16},{16,20},{20,24},{24,28},{1,5},{5,9},{9,... | collective-permute-start | bytes 9224 | tf_op jit(solution)/shard_map/ppermute | solution.py:22
  100.1 1.7 copy.66
  101.8 53.4 %while.11 = (s32[]{:T(128)}, f32[32,32,256]{2,1,0:T(8,128)S(1)}, s32[8,5]{1,0:T(8,128)S(1)}, f32[35,40,256]{2,0,1:T(8,128)}, s32[8,5]{1,0:T(8,128)S(1)}, /*index...) while((s32[]{:T(128)}, f32[32,32,256]{2,1,0:T(8,128)S(1)}, ...), condition=%wide.region_1.2_spmd.clone, body=%wide.region_0.1_spmd.clone.sunk | while | flops 146720672 | bytes 3547571 | solution.py:146
  101.8 2.0 gather_fusion
  104.7 2.4 %fusion.205 = f32[5,32,256]{2,1,0:T(8,128)S(1)} fusion(f32[5,256]{1,0:T(8,128)S(1)} %bitcast.189, f32[5,256]{1,0:T(8,128)S(1)} %bitcast.192, f32[5,256]{1,0:T(8,128)S(1)} %bitcast.190, f32[5,256]{1,0:T(8,128)S(1)} %bitcast.193, f32[5,256]{1,0:T(8,128)S(1)} %bitcast.191, f32[5,256]{1,0:T(8,128)S(1)} %bitcast.194, ...), kind=kOutput, calls=%fused_computation.22.clone.1 | convolution fusion | flops 130416640 | bytes 376832 | tf_op jit(solution)/shard_map/while/body/eval_jaxpr/vbs,bts->bvt/dot_general | solution.py:128
  108.5 2.0 gather_fusion
  111.4 2.4 %fusion.205 = f32[5,32,256]{2,1,0:T(8,128)S(1)} fusion(f32[5,256]{1,0:T(8,128)S(1)} %bitcast.189, f32[5,256]{1,0:T(8,128)S(1)} %bitcast.192, f32[5,256]{1,0:T(8,128)S(1)} %bitcast.190, f32[5,256]{1,0:T(8,128)S(1)} %bitcast.193, f32[5,256]{1,0:T(8,128)S(1)} %bitcast.191, f32[5,256]{1,0:T(8,128)S(1)} %bitcast.194, ...), kind=kOutput, calls=%fused_computation.22.clone.1 | convolution fusion | flops 130416640 | bytes 376832 | tf_op jit(solution)/shard_map/while/body/eval_jaxpr/vbs,bts->bvt/dot_general | solution.py:128
  115.2 2.0 gather_fusion
  118.0 2.4 %fusion.205 = f32[5,32,256]{2,1,0:T(8,128)S(1)} fusion(f32[5,256]{1,0:T(8,128)S(1)} %bitcast.189, f32[5,256]{1,0:T(8,128)S(1)} %bitcast.192, f32[5,256]{1,0:T(8,128)S(1)} %bitcast.190, f32[5,256]{1,0:T(8,128)S(1)} %bitcast.193, f32[5,256]{1,0:T(8,128)S(1)} %bitcast.191, f32[5,256]{1,0:T(8,128)S(1)} %bitcast.194, ...), kind=kOutput, calls=%fused_computation.22.clone.1 | convolution fusion | flops 130416640 | bytes 376832 | tf_op jit(solution)/shard_map/while/body/eval_jaxpr/vbs,bts->bvt/dot_general | solution.py:128
  121.8 2.0 gather_fusion
  124.7 2.4 %fusion.205 = f32[5,32,256]{2,1,0:T(8,128)S(1)} fusion(f32[5,256]{1,0:T(8,128)S(1)} %bitcast.189, f32[5,256]{1,0:T(8,128)S(1)} %bitcast.192, f32[5,256]{1,0:T(8,128)S(1)} %bitcast.190, f32[5,256]{1,0:T(8,128)S(1)} %bitcast.193, f32[5,256]{1,0:T(8,128)S(1)} %bitcast.191, f32[5,256]{1,0:T(8,128)S(1)} %bitcast.194, ...), kind=kOutput, calls=%fused_computation.22.clone.1 | convolution fusion | flops 130416640 | bytes 376832 | tf_op jit(solution)/shard_map/while/body/eval_jaxpr/vbs,bts->bvt/dot_general | solution.py:128
  128.5 2.0 gather_fusion
  131.4 2.4 %fusion.205 = f32[5,32,256]{2,1,0:T(8,128)S(1)} fusion(f32[5,256]{1,0:T(8,128)S(1)} %bitcast.189, f32[5,256]{1,0:T(8,128)S(1)} %bitcast.192, f32[5,256]{1,0:T(8,128)S(1)} %bitcast.190, f32[5,256]{1,0:T(8,128)S(1)} %bitcast.193, f32[5,256]{1,0:T(8,128)S(1)} %bitcast.191, f32[5,256]{1,0:T(8,128)S(1)} %bitcast.194, ...), kind=kOutput, calls=%fused_computation.22.clone.1 | convolution fusion | flops 130416640 | bytes 376832 | tf_op jit(solution)/shard_map/while/body/eval_jaxpr/vbs,bts->bvt/dot_general | solution.py:128
  135.2 2.0 gather_fusion
  138.1 2.4 %fusion.205 = f32[5,32,256]{2,1,0:T(8,128)S(1)} fusion(f32[5,256]{1,0:T(8,128)S(1)} %bitcast.189, f32[5,256]{1,0:T(8,128)S(1)} %bitcast.192, f32[5,256]{1,0:T(8,128)S(1)} %bitcast.190, f32[5,256]{1,0:T(8,128)S(1)} %bitcast.193, f32[5,256]{1,0:T(8,128)S(1)} %bitcast.191, f32[5,256]{1,0:T(8,128)S(1)} %bitcast.194, ...), kind=kOutput, calls=%fused_computation.22.clone.1 | convolution fusion | flops 130416640 | bytes 376832 | tf_op jit(solution)/shard_map/while/body/eval_jaxpr/vbs,bts->bvt/dot_general | solution.py:128
  141.9 2.0 gather_fusion
  144.7 2.4 %fusion.205 = f32[5,32,256]{2,1,0:T(8,128)S(1)} fusion(f32[5,256]{1,0:T(8,128)S(1)} %bitcast.189, f32[5,256]{1,0:T(8,128)S(1)} %bitcast.192, f32[5,256]{1,0:T(8,128)S(1)} %bitcast.190, f32[5,256]{1,0:T(8,128)S(1)} %bitcast.193, f32[5,256]{1,0:T(8,128)S(1)} %bitcast.191, f32[5,256]{1,0:T(8,128)S(1)} %bitcast.194, ...), kind=kOutput, calls=%fused_computation.22.clone.1 | convolution fusion | flops 130416640 | bytes 376832 | tf_op jit(solution)/shard_map/while/body/eval_jaxpr/vbs,bts->bvt/dot_general | solution.py:128
  148.6 2.0 gather_fusion
  151.4 2.4 %fusion.205 = f32[5,32,256]{2,1,0:T(8,128)S(1)} fusion(f32[5,256]{1,0:T(8,128)S(1)} %bitcast.189, f32[5,256]{1,0:T(8,128)S(1)} %bitcast.192, f32[5,256]{1,0:T(8,128)S(1)} %bitcast.190, f32[5,256]{1,0:T(8,128)S(1)} %bitcast.193, f32[5,256]{1,0:T(8,128)S(1)} %bitcast.191, f32[5,256]{1,0:T(8,128)S(1)} %bitcast.194, ...), kind=kOutput, calls=%fused_computation.22.clone.1 | convolution fusion | flops 130416640 | bytes 376832 | tf_op jit(solution)/shard_map/while/body/eval_jaxpr/vbs,bts->bvt/dot_general | solution.py:128
  155.2 1.6 copy.82
  172.9 1.8 convolution_bitcast_fusion.2
  174.8 3.2 %fusion.46 = f32[32,8,32]{2,1,0:T(8,128)S(1)} fusion(f32[32,32,3,32]{3,2,1,0:T(4,128)S(1)} %copy-done.1, f32[32,1,8,32]{3,2,0,1:T(8,128)S(1)} %bitcast.181, f32[32,1,8,32]{3,2,0,1:T(8,128)S(1)} %bitcast.180, f32[32,1,8,32]{3,2,0,1:T(8,128)} %bitcast.182), kind=kOutput, calls=%fused_computation.89 | convolution fusion | flops 9486336 | bytes 524288 | tf_op jit(solution)/shard_map/navr,nras->nvs/dot_general | solution.py:53
  182.2 3.1 %reduce-scatter.2.cloned.1.call-done = f32[8,8192]{1,0:T(8,128)} async-done(((f32[32,8192]{1,0:T(8,128)}), f32[8,8192]{1,0:T(8,128)}) %reduce-scatter.2.cloned.1.call-update) | async-done | bytes 262160 | tf_op jit(solution)/shard_map/reduce_scatter | solution.py:180
  187.2 21.4 %psum.7 = f32[32,8]{0,1:T(8,128)S(1)} all-reduce(f32[32,8]{0,1:T(8,128)S(1)} %convolution_bitcast_fusion.5), channel_id=1, replica_groups=mesh['leaf'=8,'vec'=4] {'leaf'}, use_global_device_ids=true, to_apply=%region_3.4 | all-reduce | flops 256 | bytes 2048 | tf_op jit(solution)/shard_map/psum | solution.py:226
  (317 shorter events, 70.3 us)
Async XLA Ops:
  7.2 76.3 %all-gather.2.cloned.1.call-start = ((), (), s32[]{:S(2)}) async-start(), calls=%async_computation.1 | async-start | bytes 1310720 | tf_op jit(solution)/shard_map/all_gather | solution.py:159
  9.5 51.9 %copy-start.11 = (f32[2,32,192]{2,1,0:T(8,128)S(1)}, f32[2,32,192]{2,1,0:T(8,128)}, u32[]{:S(2)}) copy-start(f32[2,32,192]{2,1,0:T(8,128)} %param.44) | copy-start | bytes 147460
  9.6 53.6 %copy-start.27 = (s32[4]{0:T(128)S(1)}, s32[4]{0:T(128)}, u32[]{:S(2)}) copy-start(s32[4]{0:T(128)} %constant.214) | copy-start | bytes 52
  9.6 54.2 %copy-start.26 = (s32[8]{0:T(128)S(1)}, s32[8]{0:T(128)}, u32[]{:S(2)}) copy-start(s32[8]{0:T(128)} %constant.211) | copy-start | bytes 100
  9.6 54.8 %copy-start.25 = (s32[16]{0:T(128)S(1)}, s32[16]{0:T(128)}, u32[]{:S(2)}) copy-start(s32[16]{0:T(128)} %constant.208) | copy-start | bytes 196
  9.6 55.4 %copy-start.24 = (s32[32]{0:T(128)S(1)}, s32[32]{0:T(128)}, u32[]{:S(2)}) copy-start(s32[32]{0:T(128)} %constant.205) | copy-start | bytes 388
  10.3 56.1 %copy-start.23 = (s32[2]{0:T(128)S(1)}, s32[2]{0:T(128)}, u32[]{:S(2)}) copy-start(s32[2]{0:T(128)} %constant.217) | copy-start | bytes 28
  10.3 56.1 %copy-start.21 = (s32[4]{0:T(128)S(1)}, s32[4]{0:T(128)}, u32[]{:S(2)}) copy-start(s32[4]{0:T(128)} %constant.215) | copy-start | bytes 52
  10.3 56.1 %copy-start.22 = (s32[4]{0:T(128)S(1)}, s32[4]{0:T(128)}, u32[]{:S(2)}) copy-start(s32[4]{0:T(128)} %constant.216) | copy-start | bytes 52
  10.3 56.7 %copy-start.19 = (s32[8]{0:T(128)S(1)}, s32[8]{0:T(128)}, u32[]{:S(2)}) copy-start(s32[8]{0:T(128)} %constant.212) | copy-start | bytes 100
  10.3 56.7 %copy-start.20 = (s32[8]{0:T(128)S(1)}, s32[8]{0:T(128)}, u32[]{:S(2)}) copy-start(s32[8]{0:T(128)} %constant.213) | copy-start | bytes 100
  10.3 57.3 %copy-start.17 = (s32[16]{0:T(128)S(1)}, s32[16]{0:T(128)}, u32[]{:S(2)}) copy-start(s32[16]{0:T(128)} %constant.209) | copy-start | bytes 196
  10.3 57.3 %copy-start.18 = (s32[16]{0:T(128)S(1)}, s32[16]{0:T(128)}, u32[]{:S(2)}) copy-start(s32[16]{0:T(128)} %constant.210) | copy-start | bytes 196
  10.4 57.9 %copy-start.15 = (s32[32]{0:T(128)S(1)}, s32[32]{0:T(128)}, u32[]{:S(2)}) copy-start(s32[32]{0:T(128)} %constant.206) | copy-start | bytes 388
  10.4 57.9 %copy-start.16 = (s32[32]{0:T(128)S(1)}, s32[32]{0:T(128)}, u32[]{:S(2)}) copy-start(s32[32]{0:T(128)} %constant.207) | copy-start | bytes 388
  10.4 58.5 %copy-start.13 = (s32[160]{0:T(256)S(1)}, s32[160]{0:T(256)}, u32[]{:S(2)}) copy-start(s32[160]{0:T(256)} %param.46) | copy-start | bytes 1924
  10.4 58.5 %copy-start.14 = (s32[160]{0:T(256)S(1)}, s32[160]{0:T(256)}, u32[]{:S(2)}) copy-start(s32[160]{0:T(256)} %param.45) | copy-start | bytes 1924
  11.4 67.0 %collective-permute-start.10 = (f32[2,8,32]{2,1,0:T(8,128)S(1)}, f32[2,8,32]{2,1,0:T(8,128)S(1)}, u32[]{:S(2)}, u32[]{:S(2)}) collective-permute-start(f32[2,8,32]{2,1,0:T(8,128)S(1)} %slice_add_fusion.3), channel_id=1, source_target_pairs={{0,4},{4,8},{8,12},{12,16},{16,20},{20,24},{24,28},{1,5},{5,9},{9,... | collective-permute-start | bytes 6152 | tf_op jit(solution)/shard_map/ppermute | solution.py:22
  16.3 63.7 %collective-permute-start.11 = (f32[2,8,32]{2,1,0:T(8,128)S(1)}, f32[2,8,32]{2,1,0:T(8,128)S(1)}, u32[]{:S(2)}, u32[]{:S(2)}) collective-permute-start(f32[2,8,32]{2,1,0:T(8,128)S(1)} %slice_add_fusion.3), channel_id=1, source_target_pairs={{4,0},{8,4},{12,8},{16,12},{20,16},{24,20},{28,24},{5,1},{9,5},{13... | collective-permute-start | bytes 6152 | tf_op jit(solution)/shard_map/ppermute | solution.py:25
  17.6 167.6 %reduce-scatter.2.cloned.1.call-start = ((), (), s32[]{:S(2)}) async-start(), calls=%async_computation.2 | async-start | bytes 1310720 | tf_op jit(solution)/shard_map/reduce_scatter | solution.py:180
  18.3 138.5 %collective-permute-start.8 = (f32[3,8,32]{2,1,0:T(8,128)}, f32[3,8,32]{2,1,0:T(8,128)}, u32[]{:S(2)}, u32[]{:S(2)}) collective-permute-start(f32[3,8,32]{2,1,0:T(8,128)} %get-tuple-element.113), channel_id=1, source_target_pairs={{0,4},{4,8},{8,12},{12,16},{16,20},{20,24},{24,28},{1,5},{5,9},{9,... | collective-permute-start | bytes 9224 | tf_op jit(solution)/shard_map/ppermute | solution.py:22
  24.0 60.9 %collective-permute-start.6 = (f32[3,8,32]{2,1,0:T(8,128)}, f32[3,8,32]{2,1,0:T(8,128)}, u32[]{:S(2)}, u32[]{:S(2)}) collective-permute-start(f32[3,8,32]{2,1,0:T(8,128)} %get-tuple-element.111), channel_id=1, source_target_pairs={{0,4},{4,8},{8,12},{12,16},{16,20},{20,24},{24,28},{1,5},{5,9},{9,... | collective-permute-start | bytes 9224 | tf_op jit(solution)/shard_map/ppermute | solution.py:22
  28.4 61.1 %collective-permute-start.7 = (f32[3,8,32]{2,1,0:T(8,128)}, f32[3,8,32]{2,1,0:T(8,128)}, u32[]{:S(2)}, u32[]{:S(2)}) collective-permute-start(f32[3,8,32]{2,1,0:T(8,128)} %get-tuple-element.112), channel_id=1, source_target_pairs={{4,0},{8,4},{12,8},{16,12},{20,16},{24,20},{28,24},{5,1},{9,5},{13... | collective-permute-start | bytes 9224 | tf_op jit(solution)/shard_map/ppermute | solution.py:25
  78.4 13.2 %collective-permute-start.4 = (f32[3,8,32]{2,1,0:T(8,128)}, f32[3,8,32]{2,1,0:T(8,128)S(1)}, u32[]{:S(2)}, u32[]{:S(2)}) collective-permute-start(f32[3,8,32]{2,1,0:T(8,128)} %get-tuple-element.107), channel_id=1, source_target_pairs={{0,4},{4,8},{8,12},{12,16},{16,20},{20,24},{24,28},{1,5},{5,9},{9,... | collective-permute-start | bytes 9224 | tf_op jit(solution)/shard_map/ppermute | solution.py:22
  80.0 12.9 %collective-permute-start.5 = (f32[3,8,32]{2,1,0:T(8,128)}, f32[3,8,32]{2,1,0:T(8,128)S(1)}, u32[]{:S(2)}, u32[]{:S(2)}) collective-permute-start(f32[3,8,32]{2,1,0:T(8,128)} %get-tuple-element.108), channel_id=1, source_target_pairs={{4,0},{8,4},{12,8},{16,12},{20,16},{24,20},{28,24},{5,1},{9,5},{13... | collective-permute-start | bytes 9224 | tf_op jit(solution)/shard_map/ppermute | solution.py:25
  84.9 13.1 %collective-permute-start = (f32[35,1024]{1,0:T(8,128)S(1)}, f32[35,1024]{1,0:T(8,128)S(1)}, u32[]{:S(2)}, u32[]{:S(2)}) collective-permute-start(f32[35,1024]{1,0:T(8,128)S(1)} %get-tuple-element.103), channel_id=1, source_target_pairs={{0,4},{4,8},{8,12},{12,16},{16,20},{20,24},{24,28},{1,5},{5,9},{9,... | collective-permute-start | bytes 430088 | tf_op jit(solution)/shard_map/ppermute | solution.py:22
  89.5 9.9 %collective-permute-start.1 = (f32[35,1024]{1,0:T(8,128)S(1)}, f32[35,1024]{1,0:T(8,128)S(1)}, u32[]{:S(2)}, u32[]{:S(2)}) collective-permute-start(f32[35,1024]{1,0:T(8,128)S(1)} %get-tuple-element.104), channel_id=1, source_target_pairs={{4,0},{8,4},{12,8},{16,12},{20,16},{24,20},{28,24},{5,1},{9,5},{13... | collective-permute-start | bytes 430088 | tf_op jit(solution)/shard_map/ppermute | solution.py:25
  91.6 65.3 %collective-permute-start.9 = (f32[3,8,32]{2,1,0:T(8,128)S(1)}, f32[3,8,32]{2,1,0:T(8,128)S(1)}, u32[]{:S(2)}, u32[]{:S(2)}) collective-permute-start(f32[3,8,32]{2,1,0:T(8,128)S(1)} %copy-done.12), channel_id=1, source_target_pairs={{4,0},{8,4},{12,8},{16,12},{20,16},{24,20},{28,24},{5,1},{9,5},{13... | collective-permute-start | bytes 9224 | tf_op jit(solution)/shard_map/ppermute | solution.py:25
  92.9 75.9 %collective-permute-start.2 = (f32[3,8,32]{2,1,0:T(8,128)}, f32[3,8,32]{2,1,0:T(8,128)S(1)}, u32[]{:S(2)}, u32[]{:S(2)}) collective-permute-start(f32[3,8,32]{2,1,0:T(8,128)} %get-tuple-element.105), channel_id=1, source_target_pairs={{0,4},{4,8},{8,12},{12,16},{16,20},{20,24},{24,28},{1,5},{5,9},{9,... | collective-permute-start | bytes 9224 | tf_op jit(solution)/shard_map/ppermute | solution.py:22
  98.1 70.6 %collective-permute-start.3 = (f32[3,8,32]{2,1,0:T(8,128)}, f32[3,8,32]{2,1,0:T(8,128)S(1)}, u32[]{:S(2)}, u32[]{:S(2)}) collective-permute-start(f32[3,8,32]{2,1,0:T(8,128)} %get-tuple-element.106), channel_id=1, source_target_pairs={{4,0},{8,4},{12,8},{16,12},{20,16},{24,20},{28,24},{5,1},{9,5},{13... | collective-permute-start | bytes 9224 | tf_op jit(solution)/shard_map/ppermute | solution.py:25
  157.6 17.1 %copy-start.1 = (f32[32,32,3,32]{3,2,1,0:T(4,128)S(1)}, f32[32,32,3,32]{3,2,1,0:T(4,128)}, u32[]{:S(2)}) copy-start(f32[32,32,3,32]{3,2,1,0:T(4,128)} %reshape.157) | copy-start | bytes 1179652
  186.3 22.9 %copy-start.6 = (f32[8,8192]{1,0:T(8,128)}, f32[8,8192]{1,0:T(8,128)S(1)}, u32[]{:S(2)}) copy-start(f32[8,8192]{1,0:T(8,128)S(1)} %multiply_add_fusion) | copy-start | bytes 786436
  (10 other events, 47.5 us)
Sparse Core Ops, SparseCore 0:
  17.8 19.0 all-gather.1
  157.0 28.2 reduce-scatter.1
where the time goes:
time: 217 us; the launch traced here: 216 us
  blocking collectives  52.8 us (24%)
  local copies, waits for them, and re-layouts  52.2 us (24%)
  matrix products  48 us (22%)
  starting transfers between devices  33.5 us (15%)
  between operations  15.5 us (7%)
  other arithmetic  9.62 us (4%)
  waiting for transfers between devices  3.15 us (1%)
    all_gather x1, blocking collectives, on_device(): all_roots = lax.all_gather(current, 'leaf', axis=0, tiled=True)  31.5 us
    ppermute x6, starting transfers between devices, padded_2(): lax.ppermute(lax.slice_in_dim(block, block.shape[dim] - width, None, axis...  25.7 us
    psum x1, blocking collectives, on_device(): gram_matrix = lax.psum(gram_part, 'leaf') / (leaf_count * points_dev)  21.4 us
    dot_general x8, matrix products, add_block(): jnp.einsum('vbs,bts->bvt', source_rows[:columns], kernel, precision=EXACT...  19.2 us
    gather x8, local copies, waits for them, and re-layouts, add_block(): source_rows = jnp.take(window, source_ids, axis=1)  15.9 us
    gather x15, local copies, waits for them, and re-layouts, take_rows(): gathered.append(padded[np.arange(count_nodes) + shift_by + pad_width])  15.6 us
    dot_general x8, matrix products, add_block(): jnp.einsum('qs,qhg->hsg', selection_mask, contribution, precision=EXACT_A...  10.5 us
    dot_general x5, matrix products, couple_level(): jnp.einsum('navr,nras->nvs', sources, blocks, precision=EXACT_ARITHMETIC)  7.84 us
  transfers between devices with their start and end apart: 14, of which 1 were waited for; matrix products, arithmetic and copies ran while one was open for 48% of the time, Pallas kernels for 0%

commit v1 on v0

--- a/solution.py
+++ b/solution.py
@@ -200,7 +200,27 @@
         nodes_here //= 2
     top_levels = top_ops.shape[0]
     top_fields = []
-    all_roots = lax.all_gather(current, "leaf", axis=0, tiled=True)
+    y = lax.psum(1, axis_name="leaf")
+    r_now = lax.axis_index("leaf")
+    current_block, all_values, w_next = (y, r_now, current.shape[0])
+    heap = tuple(((idx, (idx + 1) % current_block) for idx in range(current_block)))
+    all_roots = jnp.zeros(
+        (*current.shape[:0], current_block * w_next, *current.shape[1:]), current.dtype
+    )
+    all_roots = lax.dynamic_update_slice_in_dim(all_roots, current, all_values * w_next, axis=0)
+    grid = tuple(((idx, (idx - 1) % current_block) for idx in range(current_block)))
+    now = current_block // 2
+    w2 = part_next = current
+    for nth in [*range(1, now + 1)]:
+        w2 = lax.ppermute(w2, "leaf", perm=heap)
+        all_roots = lax.dynamic_update_slice_in_dim(
+            all_roots, w2, (all_values - nth) % current_block * w_next, axis=0
+        )
+        if nth < current_block - now:
+            part_next = lax.ppermute(part_next, axis_name="leaf", perm=grid)
+            all_roots = lax.dynamic_update_slice_in_dim(
+                all_roots, part_next, (all_values + nth) % current_block * w_next, axis=0
+            )
     for height in range(top_levels):
         padded_top = jnp.pad(all_roots, ((3, 3), (0, 0), (0, 0)))
         node_id = device // (1 << height)

time: 217 us -> 306 us (1.41)
  other arithmetic: 9.62 us -> 43.8 us
  waiting for transfers between devices: 3.15 us -> 35.1 us
  blocking collectives: 52.8 us -> 21.4 us
  local copies, waits for them, and re-layouts: 52.2 us -> 76.5 us
  starting transfers between devices: 33.5 us -> 49.6 us
  matrix products: 48 us -> 60.7 us
    all_gather x1 -> x0, blocking collectives: 31.5 us -> none  [on_device(): all_roots = lax.all_gather(current, 'leaf', axis=0, tiled=True)]
    reduce_scatter x1, waiting for transfers between devices: 3.09 us -> 21.8 us  [on_device(): lax.psum_scatter(partial_sum, 'vec', scatter_dimension=0, tiled=True)]
    ppermute x0 -> x7, starting transfers between devices: none -> 18.7 us  [the longest x4 12.2 us: on_device(): w2 = lax.ppermute(w2, 'leaf', perm=heap)]
    and x8, other arithmetic: 0.13 us -> 10.3 us  [add_block(): target_pts = jnp.take(local_coords, target_ids, axis=1)]
    select_n x16, other arithmetic: 0.76 us -> 10.8 us  [add_block(): source_rows = jnp.take(window, source_ids, axis=1)]
    ppermute x0 -> x7, waiting for transfers between devices: none -> 8.23 us  [the longest x3 4.85 us: on_device(): part_next = lax.ppermute(part_next, axis_name='leaf', perm=grid)]
    gather x8, local copies, waits for them, and re-layouts: 4.59 us -> 11.8 us  [add_block(): target_pts = jnp.take(local_coords, target_ids, axis=1)]
    mul x8, local copies, waits for them, and re-layouts: 0.08 us -> 5.58 us  [add_block(): (target_ids[:, None] == jnp.arange(leaves_dev)[None, :]).astype(jnp.float32)]
  transfers between devices with their start and end apart: 14 -> 21, of which waited for: 1 -> 6; matrix products, arithmetic and copies ran while one was open for 48% -> 22% of each run, Pallas kernels for 0% -> 0%
where the time goes in v1:
time: 306 us; the launch traced here: 303 us
  local copies, waits for them, and re-layouts  76.5 us (25%)
  matrix products  60.7 us (20%)
  starting transfers between devices  49.6 us (16%)
  other arithmetic  43.8 us (14%)
  waiting for transfers between devices  35.1 us (11%)
  blocking collectives  21.4 us (7%)
  between operations  15.6 us (5%)
    ppermute x6, starting transfers between devices, padded_2(): lax.ppermute(lax.slice_in_dim(block, block.shape[dim] - width, None, axis...  22.9 us
    reduce_scatter x1, waiting for transfers between devices, on_device(): lax.psum_scatter(partial_sum, 'vec', scatter_dimension=0, tiled=True)  21.8 us
    psum x1, blocking collectives, on_device(): gram_matrix = lax.psum(gram_part, 'leaf') / (leaf_count * points_dev)  21.4 us
    dot_general x8, matrix products, add_block(): jnp.einsum('vbs,bts->bvt', source_rows[:columns], kernel, precision=EXACT...  19.2 us
    gather x15, local copies, waits for them, and re-layouts, take_rows(): gathered.append(padded[np.arange(count_nodes) + shift_by + pad_width])  17.1 us
    dot_general x8, matrix products, add_block(): jnp.einsum('qs,qhg->hsg', selection_mask, contribution, precision=EXACT_A...  15.9 us
    gather x8, local copies, waits for them, and re-layouts, add_block(): source_rows = jnp.take(window, source_ids, axis=1)  15.9 us
    ppermute x4, starting transfers between devices, on_device(): w2 = lax.ppermute(w2, 'leaf', perm=heap)  12.2 us
  transfers between devices with their start and end apart: 21, of which 6 were waited for; matrix products, arithmetic and copies ran while one was open for 22% of the time, Pallas kernels for 0%

profile of v1, /device:TPU:0, one launch (start us, length us, event | category | flops | bytes accessed | tf_op | source)
XLA Modules:
  0.0 303.4 jit_solution(16750920427987566096)
XLA Ops:
  7.2 2.3 fusion.55
  12.1 3.0 collective-permute-start.12
  15.0 3.0 %collective-permute-start.13 = (f32[1,8,32]{2,1,0:T(8,128)}, f32[1,8,32]{2,1,0:T(8,128)}, u32[]{:S(2)}, u32[]{:S(2)}) collective-permute-start(f32[1,8,32]{2,1,0:T(8,128)} %get-tuple-element.88), channel_id=1, source_target_pairs={{0,28},{4,0},{8,4},{12,8},{16,12},{20,16},{24,20},{28,24},{1,29},{... | collective-permute-start | bytes 3080 | tf_op jit(solution)/shard_map/ppermute | solution.py:220
  21.9 4.7 %collective-permute-start.8 = (f32[3,8,32]{2,1,0:T(8,128)}, f32[3,8,32]{2,1,0:T(8,128)S(1)}, u32[]{:S(2)}, u32[]{:S(2)}) collective-permute-start(f32[3,8,32]{2,1,0:T(8,128)} %get-tuple-element.108), channel_id=1, source_target_pairs={{0,4},{4,8},{8,12},{12,16},{16,20},{20,24},{24,28},{1,5},{5,9},{9,... | collective-permute-start | bytes 9224 | tf_op jit(solution)/shard_map/ppermute | solution.py:22
  42.4 3.2 %reshape.157 = f32[32,32,3,32]{3,2,1,0:T(4,128)} reshape(f32[32,32,96]{2,1,0:T(8,128)} %slice.211) | data formatting | bytes 786432 | tf_op jit(solution)/shard_map/reshape | solution.py:52
  52.5 4.9 %collective-permute-start.6 = (f32[3,8,32]{2,1,0:T(8,128)S(1)}, f32[3,8,32]{2,1,0:T(8,128)S(1)}, u32[]{:S(2)}, u32[]{:S(2)}) collective-permute-start(f32[3,8,32]{2,1,0:T(8,128)S(1)} %copy-done.23), channel_id=1, source_target_pairs={{0,4},{4,8},{8,12},{12,16},{16,20},{20,24},{24,28},{1,5},{5,9},{9,... | collective-permute-start | bytes 9224 | tf_op jit(solution)/shard_map/ppermute | solution.py:22
  59.4 3.6 %collective-permute-start.14 = (f32[1,8,32]{2,1,0:T(8,128)}, f32[1,8,32]{2,1,0:T(8,128)S(1)}, u32[]{:S(2)}, u32[]{:S(2)}) collective-permute-start(f32[1,8,32]{2,1,0:T(8,128)} %collective-permute-done.12), channel_id=1, source_target_pairs={{0,4},{4,8},{8,12},{12,16},{16,20},{20,24},{24,28},{28,0},{1,5},{5... | collective-permute-start | bytes 3080 | tf_op jit(solution)/shard_map/ppermute | solution.py:215
  67.6 2.2 collective-permute-start.15
  69.7 2.5 collective-permute-done.15
  72.3 2.9 collective-permute-start.16
  75.2 3.4 %collective-permute-done.16 = f32[1,8,32]{2,1,0:T(8,128)S(1)} collective-permute-done((f32[1,8,32]{2,1,0:T(8,128)S(1)}, f32[1,8,32]{2,1,0:T(8,128)S(1)}, u32[]{:S(2)}, u32[]{:S(2)}) %collective-permute-start.16) | collective-permute-done | bytes 1056 | tf_op jit(solution)/shard_map/ppermute | solution.py:215
  79.9 2.3 collective-permute-done.17
  82.2 3.6 %collective-permute-start.4 = (f32[3,8,32]{2,1,0:T(8,128)}, f32[3,8,32]{2,1,0:T(8,128)}, u32[]{:S(2)}, u32[]{:S(2)}) collective-permute-start(f32[3,8,32]{2,1,0:T(8,128)} %get-tuple-element.102), channel_id=1, source_target_pairs={{0,4},{4,8},{8,12},{12,16},{16,20},{20,24},{24,28},{1,5},{5,9},{9,... | collective-permute-start | bytes 9224 | tf_op jit(solution)/shard_map/ppermute | solution.py:22
  87.7 4.5 %collective-permute-start.2 = (f32[3,8,32]{2,1,0:T(8,128)}, f32[3,8,32]{2,1,0:T(8,128)S(1)}, u32[]{:S(2)}, u32[]{:S(2)}) collective-permute-start(f32[3,8,32]{2,1,0:T(8,128)} %get-tuple-element.100), channel_id=1, source_target_pairs={{0,4},{4,8},{8,12},{12,16},{16,20},{20,24},{24,28},{1,5},{5,9},{9,... | collective-permute-start | bytes 9224 | tf_op jit(solution)/shard_map/ppermute | solution.py:22
  94.3 2.7 collective-permute-start.18
  109.6 2.4 convolution_bitcast_fusion.2
  112.0 4.7 %fusion.46 = f32[32,8,32]{2,1,0:T(8,128)} fusion(f32[32,32,3,32]{3,2,1,0:T(4,128)} %reshape.157, f32[32,1,8,32]{3,2,0,1:T(8,128)} %bitcast.181, f32[32,1,8,32]{3,2,0,1:T(8,128)} %bitcast.180, f32[32,1,8,32]{3,2,0,1:T(8,128)} %bitcast.182), kind=kOutput, calls=%fused_computation.89 | convolution fusion | flops 9486336 | bytes 524288 | tf_op jit(solution)/shard_map/navr,nras->nvs/dot_general | solution.py:53
  129.8 3.3 %collective-permute-start = (f32[35,1024]{1,0:T(8,128)S(1)}, f32[35,1024]{1,0:T(8,128)S(1)}, u32[]{:S(2)}, u32[]{:S(2)}) collective-permute-start(f32[35,1024]{1,0:T(8,128)S(1)} %get-tuple-element.98), channel_id=1, source_target_pairs={{0,4},{4,8},{8,12},{12,16},{16,20},{20,24},{24,28},{1,5},{5,9},{9,... | collective-permute-start | bytes 430088 | tf_op jit(solution)/shard_map/ppermute | solution.py:22
  135.9 4.4 %collective-permute-done.1 = f32[35,1024]{1,0:T(8,128)S(1)} collective-permute-done((f32[35,1024]{1,0:T(8,128)S(1)}, f32[35,1024]{1,0:T(8,128)S(1)}, u32[]{:S(2)}, u32[]{:S(2)}) %collective-permute-start.1) | collective-permute-done | bytes 143392 | tf_op jit(solution)/shard_map/ppermute | solution.py:25
  142.7 101.5 %while.11 = (s32[]{:T(128)}, f32[32,32,256]{2,1,0:T(8,128)S(1)}, s32[8,5]{1,0:T(8,128)}, f32[35,40,256]{2,0,1:T(8,128)}, s32[8,5]{1,0:T(8,128)}, /*index=5*/f32[...) while((s32[]{:T(128)}, f32[32,32,256]{2,1,0:T(8,128)S(1)}, s32[8,5]{1,0:T(8,128)}, ...), condition=%wide.region_1.2_spmd.clone, body=%wide.region_0.1_spmd.clone.sunk | while | flops 146720672 | bytes 3547571 | solution.py:146
  150.3 2.4 fusion.197
  153.4 2.0 fusion.199
  163.0 2.4 fusion.197
  175.6 2.4 fusion.197
  188.3 2.4 fusion.197
  201.0 2.4 fusion.197
  213.7 2.4 fusion.197
  226.4 2.4 fusion.197
  229.5 2.0 fusion.199
  239.1 2.4 fusion.197
  250.8 21.8 %reduce-scatter.2.cloned.1.call-done = f32[8,8192]{1,0:T(8,128)} async-done(((f32[32,8192]{1,0:T(8,128)}), f32[8,8192]{1,0:T(8,128)}) %reduce-scatter.2.cloned.1.call-update) | async-done | bytes 262160 | tf_op jit(solution)/shard_map/reduce_scatter | solution.py:180
  274.5 21.4 %psum.7 = f32[32,8]{0,1:T(8,128)S(1)} all-reduce(f32[32,8]{0,1:T(8,128)S(1)} %convolution_bitcast_fusion.5), channel_id=1, replica_groups=mesh['leaf'=8,'vec'=4] {'leaf'}, use_global_device_ids=true, to_apply=%region_3.4 | all-reduce | flops 256 | bytes 2048 | tf_op jit(solution)/shard_map/psum | solution.py:246
  (360 shorter events, 156.9 us)
Async XLA Ops:
  7.2 120.3 %all-gather.2.cloned.1.call-start = ((), (), s32[]{:S(2)}) async-start(), calls=%async_computation.1 | async-start | bytes 1310720 | tf_op jit(solution)/shard_map/all_gather | solution.py:159
  10.7 19.7 %copy-start.7 = (f32[8,8,32]{2,1,0:T(8,128)}, f32[8,8,32]{2,1,0:T(8,128)S(1)}, u32[]{:S(2)}) copy-start(f32[8,8,32]{2,1,0:T(8,128)S(1)} %slice_add_fusion.1) | copy-start | bytes 24580
  12.1 38.5 %collective-permute-start.12 = (f32[1,8,32]{2,1,0:T(8,128)}, f32[1,8,32]{2,1,0:T(8,128)}, u32[]{:S(2)}, u32[]{:S(2)}) collective-permute-start(f32[1,8,32]{2,1,0:T(8,128)} %get-tuple-element.88), channel_id=1, source_target_pairs={{0,4},{4,8},{8,12},{12,16},{16,20},{20,24},{24,28},{28,0},{1,5},{5... | collective-permute-start | bytes 3080 | tf_op jit(solution)/shard_map/ppermute | solution.py:215
  15.0 37.5 %collective-permute-start.13 = (f32[1,8,32]{2,1,0:T(8,128)}, f32[1,8,32]{2,1,0:T(8,128)}, u32[]{:S(2)}, u32[]{:S(2)}) collective-permute-start(f32[1,8,32]{2,1,0:T(8,128)} %get-tuple-element.88), channel_id=1, source_target_pairs={{0,28},{4,0},{8,4},{12,8},{16,12},{20,16},{24,20},{28,24},{1,29},{... | collective-permute-start | bytes 3080 | tf_op jit(solution)/shard_map/ppermute | solution.py:220
  18.1 40.0 %collective-permute-start.10 = (f32[2,8,32]{2,1,0:T(8,128)S(1)}, f32[2,8,32]{2,1,0:T(8,128)}, u32[]{:S(2)}, u32[]{:S(2)}) collective-permute-start(f32[2,8,32]{2,1,0:T(8,128)S(1)} %slice_add_fusion.3), channel_id=1, source_target_pairs={{0,4},{4,8},{8,12},{12,16},{16,20},{20,24},{24,28},{1,5},{5,9},{9,... | collective-permute-start | bytes 6152 | tf_op jit(solution)/shard_map/ppermute | solution.py:22
  19.9 39.4 %collective-permute-start.11 = (f32[2,8,32]{2,1,0:T(8,128)S(1)}, f32[2,8,32]{2,1,0:T(8,128)}, u32[]{:S(2)}, u32[]{:S(2)}) collective-permute-start(f32[2,8,32]{2,1,0:T(8,128)S(1)} %slice_add_fusion.3), channel_id=1, source_target_pairs={{4,0},{8,4},{12,8},{16,12},{20,16},{24,20},{28,24},{5,1},{9,5},{13... | collective-permute-start | bytes 6152 | tf_op jit(solution)/shard_map/ppermute | solution.py:25
  21.3 251.3 %reduce-scatter.2.cloned.1.call-start = ((), (), s32[]{:S(2)}) async-start(), calls=%async_computation.2 | async-start | bytes 1310720 | tf_op jit(solution)/shard_map/reduce_scatter | solution.py:180
  21.9 71.0 %collective-permute-start.8 = (f32[3,8,32]{2,1,0:T(8,128)}, f32[3,8,32]{2,1,0:T(8,128)S(1)}, u32[]{:S(2)}, u32[]{:S(2)}) collective-permute-start(f32[3,8,32]{2,1,0:T(8,128)} %get-tuple-element.108), channel_id=1, source_target_pairs={{0,4},{4,8},{8,12},{12,16},{16,20},{20,24},{24,28},{1,5},{5,9},{9,... | collective-permute-start | bytes 9224 | tf_op jit(solution)/shard_map/ppermute | solution.py:22
  26.7 10.4 %copy-start.28 = (s32[16]{0:T(128)S(1)}, s32[16]{0:T(128)}, u32[]{:S(2)}) copy-start(s32[16]{0:T(128)} %constant.253) | copy-start | bytes 196
  26.8 10.9 %copy-start.26 = (s32[32]{0:T(128)S(1)}, s32[32]{0:T(128)}, u32[]{:S(2)}) copy-start(s32[32]{0:T(128)} %constant.250) | copy-start | bytes 388
  26.8 10.9 %copy-start.27 = (s32[32]{0:T(128)S(1)}, s32[32]{0:T(128)}, u32[]{:S(2)}) copy-start(s32[32]{0:T(128)} %constant.251) | copy-start | bytes 388
  26.8 11.5 %copy-start.24 = (s32[160]{0:T(256)S(1)}, s32[160]{0:T(256)}, u32[]{:S(2)}) copy-start(s32[160]{0:T(256)} %param.46) | copy-start | bytes 1924
  26.8 11.5 %copy-start.25 = (s32[160]{0:T(256)S(1)}, s32[160]{0:T(256)}, u32[]{:S(2)}) copy-start(s32[160]{0:T(256)} %param.45) | copy-start | bytes 1924
  45.6 12.5 %copy-start.22 = (f32[3,8,32]{2,1,0:T(8,128)S(1)}, f32[3,8,32]{2,1,0:T(8,128)}, u32[]{:S(2)}) copy-start(f32[3,8,32]{2,1,0:T(8,128)} %get-tuple-element.107) | copy-start | bytes 9220
  45.6 46.6 %copy-start.8 = (f32[8,8,32]{2,1,0:T(8,128)S(1)}, f32[8,8,32]{2,1,0:T(8,128)}, u32[]{:S(2)}) copy-start(f32[8,8,32]{2,1,0:T(8,128)} %copy-done.7) | copy-start | bytes 24580
  50.5 43.8 %collective-permute-start.9 = (f32[3,8,32]{2,1,0:T(8,128)}, f32[3,8,32]{2,1,0:T(8,128)S(1)}, u32[]{:S(2)}, u32[]{:S(2)}) collective-permute-start(f32[3,8,32]{2,1,0:T(8,128)} %get-tuple-element.109), channel_id=1, source_target_pairs={{4,0},{8,4},{12,8},{16,12},{20,16},{24,20},{28,24},{5,1},{9,5},{13... | collective-permute-start | bytes 9224 | tf_op jit(solution)/shard_map/ppermute | solution.py:25
  52.5 33.3 %collective-permute-start.6 = (f32[3,8,32]{2,1,0:T(8,128)S(1)}, f32[3,8,32]{2,1,0:T(8,128)S(1)}, u32[]{:S(2)}, u32[]{:S(2)}) collective-permute-start(f32[3,8,32]{2,1,0:T(8,128)S(1)} %copy-done.23), channel_id=1, source_target_pairs={{0,4},{4,8},{8,12},{12,16},{16,20},{20,24},{24,28},{1,5},{5,9},{9,... | collective-permute-start | bytes 9224 | tf_op jit(solution)/shard_map/ppermute | solution.py:22
  58.1 29.0 %collective-permute-start.7 = (f32[3,8,32]{2,1,0:T(8,128)S(1)}, f32[3,8,32]{2,1,0:T(8,128)S(1)}, u32[]{:S(2)}, u32[]{:S(2)}) collective-permute-start(f32[3,8,32]{2,1,0:T(8,128)S(1)} %copy-done.22), channel_id=1, source_target_pairs={{4,0},{8,4},{12,8},{16,12},{20,16},{24,20},{28,24},{5,1},{9,5},{13... | collective-permute-start | bytes 9224 | tf_op jit(solution)/shard_map/ppermute | solution.py:25
  59.4 8.2 %collective-permute-start.14 = (f32[1,8,32]{2,1,0:T(8,128)}, f32[1,8,32]{2,1,0:T(8,128)S(1)}, u32[]{:S(2)}, u32[]{:S(2)}) collective-permute-start(f32[1,8,32]{2,1,0:T(8,128)} %collective-permute-done.12), channel_id=1, source_target_pairs={{0,4},{4,8},{8,12},{12,16},{16,20},{20,24},{24,28},{28,0},{1,5},{5... | collective-permute-start | bytes 3080 | tf_op jit(solution)/shard_map/ppermute | solution.py:215
  67.6 4.7 %collective-permute-start.15 = (f32[1,8,32]{2,1,0:T(8,128)}, f32[1,8,32]{2,1,0:T(8,128)S(1)}, u32[]{:S(2)}, u32[]{:S(2)}) collective-permute-start(f32[1,8,32]{2,1,0:T(8,128)} %collective-permute-done.13), channel_id=1, source_target_pairs={{0,28},{4,0},{8,4},{12,8},{16,12},{20,16},{24,20},{28,24},{1,29},{... | collective-permute-start | bytes 3080 | tf_op jit(solution)/shard_map/ppermute | solution.py:220
  72.3 6.3 %collective-permute-start.16 = (f32[1,8,32]{2,1,0:T(8,128)S(1)}, f32[1,8,32]{2,1,0:T(8,128)S(1)}, u32[]{:S(2)}, u32[]{:S(2)}) collective-permute-start(f32[1,8,32]{2,1,0:T(8,128)S(1)} %collective-permute-done.14), channel_id=1, source_target_pairs={{0,4},{4,8},{8,12},{12,16},{16,20},{20,24},{24,28},{28,0},{1,5},{5... | collective-permute-start | bytes 3080 | tf_op jit(solution)/shard_map/ppermute | solution.py:215
  78.6 3.6 %collective-permute-start.17 = (f32[1,8,32]{2,1,0:T(8,128)S(1)}, f32[1,8,32]{2,1,0:T(8,128)S(1)}, u32[]{:S(2)}, u32[]{:S(2)}) collective-permute-start(f32[1,8,32]{2,1,0:T(8,128)S(1)} %collective-permute-done.15), channel_id=1, source_target_pairs={{0,28},{4,0},{8,4},{12,8},{16,12},{20,16},{24,20},{28,24},{1,29},{... | collective-permute-start | bytes 3080 | tf_op jit(solution)/shard_map/ppermute | solution.py:220
  82.2 35.5 %collective-permute-start.4 = (f32[3,8,32]{2,1,0:T(8,128)}, f32[3,8,32]{2,1,0:T(8,128)}, u32[]{:S(2)}, u32[]{:S(2)}) collective-permute-start(f32[3,8,32]{2,1,0:T(8,128)} %get-tuple-element.102), channel_id=1, source_target_pairs={{0,4},{4,8},{8,12},{12,16},{16,20},{20,24},{24,28},{1,5},{5,9},{9,... | collective-permute-start | bytes 9224 | tf_op jit(solution)/shard_map/ppermute | solution.py:22
  85.8 31.9 %collective-permute-start.5 = (f32[3,8,32]{2,1,0:T(8,128)}, f32[3,8,32]{2,1,0:T(8,128)}, u32[]{:S(2)}, u32[]{:S(2)}) collective-permute-start(f32[3,8,32]{2,1,0:T(8,128)} %get-tuple-element.103), channel_id=1, source_target_pairs={{4,0},{8,4},{12,8},{16,12},{20,16},{24,20},{28,24},{5,1},{9,5},{13... | collective-permute-start | bytes 9224 | tf_op jit(solution)/shard_map/ppermute | solution.py:25
  87.7 16.4 %collective-permute-start.2 = (f32[3,8,32]{2,1,0:T(8,128)}, f32[3,8,32]{2,1,0:T(8,128)S(1)}, u32[]{:S(2)}, u32[]{:S(2)}) collective-permute-start(f32[3,8,32]{2,1,0:T(8,128)} %get-tuple-element.100), channel_id=1, source_target_pairs={{0,4},{4,8},{8,12},{12,16},{16,20},{20,24},{24,28},{1,5},{5,9},{9,... | collective-permute-start | bytes 9224 | tf_op jit(solution)/shard_map/ppermute | solution.py:22
  93.0 11.7 %collective-permute-start.3 = (f32[3,8,32]{2,1,0:T(8,128)}, f32[3,8,32]{2,1,0:T(8,128)}, u32[]{:S(2)}, u32[]{:S(2)}) collective-permute-start(f32[3,8,32]{2,1,0:T(8,128)} %get-tuple-element.101), channel_id=1, source_target_pairs={{4,0},{8,4},{12,8},{16,12},{20,16},{24,20},{28,24},{5,1},{9,5},{13... | collective-permute-start | bytes 9224 | tf_op jit(solution)/shard_map/ppermute | solution.py:25
  94.3 28.1 %collective-permute-start.18 = (f32[1,8,32]{2,1,0:T(8,128)S(1)}, f32[1,8,32]{2,1,0:T(8,128)S(1)}, u32[]{:S(2)}, u32[]{:S(2)}) collective-permute-start(f32[1,8,32]{2,1,0:T(8,128)S(1)} %collective-permute-done.16), channel_id=1, source_target_pairs={{0,4},{4,8},{8,12},{12,16},{16,20},{20,24},{24,28},{28,0},{1,5},{5... | collective-permute-start | bytes 3080 | tf_op jit(solution)/shard_map/ppermute | solution.py:215
  129.8 6.1 %collective-permute-start = (f32[35,1024]{1,0:T(8,128)S(1)}, f32[35,1024]{1,0:T(8,128)S(1)}, u32[]{:S(2)}, u32[]{:S(2)}) collective-permute-start(f32[35,1024]{1,0:T(8,128)S(1)} %get-tuple-element.98), channel_id=1, source_target_pairs={{0,4},{4,8},{8,12},{12,16},{16,20},{20,24},{24,28},{1,5},{5,9},{9,... | collective-permute-start | bytes 430088 | tf_op jit(solution)/shard_map/ppermute | solution.py:22
  133.1 7.2 %collective-permute-start.1 = (f32[35,1024]{1,0:T(8,128)S(1)}, f32[35,1024]{1,0:T(8,128)S(1)}, u32[]{:S(2)}, u32[]{:S(2)}) collective-permute-start(f32[35,1024]{1,0:T(8,128)S(1)} %get-tuple-element.99), channel_id=1, source_target_pairs={{4,0},{8,4},{12,8},{16,12},{20,16},{24,20},{28,24},{5,1},{9,5},{13... | collective-permute-start | bytes 430088 | tf_op jit(solution)/shard_map/ppermute | solution.py:25
  249.1 23.5 %copy-start.3 = (f32[8,8192]{1,0:T(8,128)S(1)}, f32[8,8192]{1,0:T(8,128)}, u32[]{:S(2)}) copy-start(f32[8,8192]{1,0:T(8,128)} %param.40) | copy-start | bytes 786436
  250.1 23.5 %copy-start.1 = (f32[32,8192]{1,0:T(8,128)S(1)}, f32[32,8192]{1,0:T(8,128)}, u32[]{:S(2)}) copy-start(f32[32,8192]{1,0:T(8,128)} %all-gather.2.cloned.1.call-done) | copy-start | bytes 3145732
  273.6 22.9 %copy-start.4 = (f32[8,8192]{1,0:T(8,128)}, f32[8,8192]{1,0:T(8,128)S(1)}, u32[]{:S(2)}) copy-start(f32[8,8192]{1,0:T(8,128)S(1)} %multiply_add_fusion) | copy-start | bytes 786436
  (28 other events, 153.2 us)
Sparse Core Ops, SparseCore 0:
  21.4 18.9 all-gather.1
  246.1 26.5 reduce-scatter.1
